TPU v7x, 128 devices: a whole 4x4x4 slice. The times are simulated.
128 devices in a mesh: gx: 16 (over x, y), gy: 8 (over z, core).
Axes of the slice: x: 4, y: 4, z: 4, core: 2. Of those that a mesh axis runs over, the one named last changes fastest.
Arguments:
- fields: float32 [4, 4, 640, 20480], P(None, None, 'gy', 'gx'), may hold values from -6 to 6
- owner: int32 [8192, 1], P(('gx', 'gy')), may hold values from 0 to 127; in each aligned block of 64 rows (0 to 63, 64 to 127, ...) at most 2 rows name the same one
Outputs:
- received: float32 [32768, 640], P(('gx', 'gy'))
Inputs may be any that keep to these rules, and one draw needn't show every extreme that they name: Among the blocks of one device, no owner is named more than 2 times, a bound that some block reaches.
All inputs are finite; a program needn't handle non-finite values.
Results may differ from a plain program's by a relative error of at most 0.0001.
Values sent between devices are 32-bit elements; how exact they have to be, the bound alone decides.
A program may use at most 256 MiB of HBM per device.

v0:
```python
import functools

import jax
import jax.numpy as jnp
import numpy as np
from jax import lax
from jax.experimental import pallas as pl
from jax.experimental.pallas import tpu as pltpu
from jax.sharding import PartitionSpec as P

MESH = pl.DeviceIdType.MESH
BLK = 4
LEV = 4
RATIO = 10
TAPS = 21
SIGMA_CELLS = 2.8867513
PAIRS = ((0, 0), (0, 1), (0, 2), (0, 3), (1, 1), (1, 2), (1, 3), (2, 2), (2, 3), (3, 3))
NF = 4 + len(PAIRS)
FL = NF * LEV
MAIN = FL * 8
SIDE = 64
ROWS = MAIN + 2 * SIDE
KC = 256
ORDER = (0, 3, 1, 2)
LANE_LAST = 63


def gauss_taps():
    spread = np.arange(TAPS, dtype=np.float32) - np.float32(10.0)
    values = np.exp(-spread * spread / np.float32(2.0 * SIGMA_CELLS * SIGMA_CELLS)).astype(np.float32)
    return (values / values.sum(dtype=np.float32)).astype(np.float32)


def east_matrix(length, taps):
    coarse = length // RATIO
    w = np.zeros((length, 256), np.float32)
    cols = [(128, coarse), (128 + LANE_LAST, -1)]
    for lane in range(128):
        cols.append((lane, 4 * (lane % 32) + ORDER[lane // 32]))
    for lane, j in cols:
        for t in range(TAPS):
            x = RATIO * j - 5 + t
            if 0 <= x < length:
                w[x, lane] = taps[t]
    return w


def block_matrix():
    m = np.zeros((256, 256), np.float32)
    for grp in range(4):
        for kl in range(8):
            for i in range(8):
                by, r = divmod(i, 4)
                m[grp * 64 + kl * 8 + i, by * 128 + kl * 16 + r * 4 + ORDER[grp]] = 1.0
    return m


def split3(x):
    hi = x.astype(jnp.bfloat16)
    rest = x - hi.astype(jnp.float32)
    mid = rest.astype(jnp.bfloat16)
    lo = (rest - mid.astype(jnp.float32)).astype(jnp.bfloat16)
    return hi, mid, lo


def iota(shape, dim):
    return lax.broadcasted_iota(jnp.int32, shape, dim)


def north_parts(v, g):
    q5, q0 = g[5] * v[0], g[0] * v[5]
    a = q5 + g[10] * v[5] + g[9] * (v[4] + v[6]) + g[8] * (v[3] + v[7]) + g[7] * (v[2] + v[8]) + g[6] * (v[1] + v[9])
    b = q0 + g[1] * v[6] + g[2] * v[7] + g[3] * v[8] + g[4] * v[9]
    c = q5 + q0 + g[4] * v[1] + g[3] * v[2] + g[2] * v[3] + g[1] * v[4]
    return a, b, c


def north_chunk(f_ref, kc, x_ref, g):
    row = iota((8, 128), 0)
    for lev in range(LEV):
        for lt in range(KC // 128):
            lanes = slice(lt * 128, lt * 128 + 128)
            x = [[f_ref[kc * (KC // 128) + lt, a, lev, pl.ds(o, 8, stride=RATIO), :] for o in range(RATIO)] for a in range(4)]
            for f in range(NF):
                if f < 4:
                    v = x[f]
                else:
                    p, q = PAIRS[f - 4]
                    v = [x[p][o] * x[q][o] for o in range(RATIO)]
                a, b, c = north_parts(v, g)
                b = pltpu.roll(b, 1, 0)
                c = pltpu.roll(c, 7, 0)
                fl = f * LEV + lev
                x_ref[fl * 8 : fl * 8 + 8, lanes] = a + jnp.where(row == 0, 0.0, b) + jnp.where(row == 7, 0.0, c)
                x_ref[MAIN + fl : MAIN + fl + 1, lanes] = b[0:1]
                x_ref[MAIN + SIDE + fl : MAIN + SIDE + fl + 1, lanes] = c[7:8]


def selector(owner_ref):
    own = owner_ref[...].astype(jnp.float32)
    row = jnp.broadcast_to(jnp.concatenate([own, own], axis=1), (128, 128))
    col = row.T[:64]
    before = (col == row[:64]) & (iota((64, 128), 0) < (iota((64, 128), 1) & 63))
    rank = jnp.sum(before.astype(jnp.float32), axis=0, keepdims=True)
    slot = row[0:1] * 2.0 + rank
    where = iota((256, 128), 0).astype(jnp.float32)
    return (where == slot).astype(jnp.bfloat16)


def kernel(n_gx, n_gy, g, f_hbm, w_hbm, m_hbm, o_hbm, dst, f_ref, w_ref, m_ref, owner_ref, x_ref, t_ref, s_ref, src,
           edge, corner, r_next, r_prev, r_side, r_corner, fsem, wsem, msem, osem, ssem, rsem, hsend, hrecv, lsem):
    n = n_gx * n_gy
    gx, gy = lax.axis_index("gx"), lax.axis_index("gy")
    me = gx * n_gy + gy
    steps = w_ref.shape[0]
    per = KC // 128

    def f_copy(lt):
        return pltpu.make_async_copy(f_hbm.at[:, :, :, pl.ds(pl.multiple_of(lt * 128, 128), 128)], f_ref.at[lt], fsem.at[lt])

    def w_copy(kc):
        return pltpu.make_async_copy(w_hbm.at[pl.ds(pl.multiple_of(kc * KC, KC), KC)], w_ref.at[kc], wsem.at[kc])

    for kc in range(steps):
        for lt in range(per):
            f_copy(kc * per + lt).start()
        w_copy(kc).start()
    m_copy = pltpu.make_async_copy(m_hbm, m_ref, msem)
    m_copy.start()
    o_copy = pltpu.make_async_copy(o_hbm, owner_ref, osem)
    o_copy.start()

    barrier = pltpu.get_barrier_semaphore()

    def greet(k, carry):
        d = lax.rem(me + k, n)
        pl.semaphore_signal(barrier, inc=1, device_id=(d // n_gy, lax.rem(d, n_gy)), device_id_type=MESH)
        return carry

    lax.fori_loop(1, n, greet, 0)
    x_ref[MAIN:ROWS] = jnp.zeros((2 * SIDE, KC), jnp.float32)
    t_ref[...] = jnp.zeros_like(t_ref)

    def chunk(kc, carry):
        for lt in range(per):
            f_copy(kc * per + lt).wait()
        north_chunk(f_ref, kc, x_ref, g)
        w_copy(kc).wait()
        t_ref[...] += jnp.dot(
            x_ref[...], w_ref[kc], precision=lax.Precision.HIGHEST, preferred_element_type=jnp.float32)
        return carry

    lax.fori_loop(0, steps, chunk, 0)

    lane = iota((8, 128), 1)
    row = iota((8, 128), 0)
    keep = (lane == 0) | (lane == LANE_LAST)
    packed = jnp.zeros((8, 128), jnp.float32)
    for fl in range(FL):
        v = jnp.where(keep, t_ref[fl * 8 : fl * 8 + 8, 128:256], 0.0)
        packed = packed + (pltpu.roll(v, fl, 1) if fl else v)
    edge[...] = packed
    turned = t_ref[MAIN:ROWS, 128:256].T
    corner[...] = jnp.where(row == 0, turned[0:1], turned[LANE_LAST : LANE_LAST + 1])

    pl.semaphore_wait(barrier, n - 1)
    east, west = lax.rem(gx + 1, n_gx), lax.rem(gx + n_gx - 1, n_gx)
    up, down = lax.rem(gy + 1, n_gy), lax.rem(gy + n_gy - 1, n_gy)
    moves = (
        (t_ref.at[MAIN : MAIN + SIDE, 0:128], r_next, (gx, up)),
        (t_ref.at[MAIN + SIDE : ROWS, 0:128], r_prev, (gx, down)),
        (edge, r_side.at[0], (east, gy)),
        (edge, r_side.at[1], (west, gy)),
        (corner, r_corner.at[0], (east, up)),
        (corner, r_corner.at[1], (east, down)),
        (corner, r_corner.at[2], (west, up)),
        (corner, r_corner.at[3], (west, down)),
    )
    copies = [
        pltpu.make_async_remote_copy(s, d, hsend.at[i], hrecv.at[i], device_id=to, device_id_type=MESH)
        for i, (s, d, to) in enumerate(moves)
    ]
    for copy in copies:
        copy.start()
    o_copy.wait()
    sel = selector(owner_ref)
    for copy in copies:
        copy.wait()

    side = jnp.where(lane < 60, r_side[0], r_side[1])
    c0, c1, c2, c3 = r_corner[0], r_corner[1], r_corner[2], r_corner[3]
    first = (lane < FL)
    secnd = (lane >= LANE_LAST) & (lane < LANE_LAST + FL)
    side = side + jnp.where(first & (row == 0), c0, 0.0)
    side = side + jnp.where(first & (row == 7), pltpu.roll(jnp.broadcast_to(c1[0:1], (8, 128)), 64, 1), 0.0)
    side = side + jnp.where(secnd & (row == 0), pltpu.roll(jnp.broadcast_to(c2[1:2], (8, 128)), LANE_LAST, 1), 0.0)
    side = side + jnp.where(secnd & (row == 7), pltpu.roll(jnp.broadcast_to(c3[1:2], (8, 128)), 127, 1), 0.0)
    for lev in range(LEV):
        m = []
        for f in range(NF):
            fl = f * LEV + lev
            v = t_ref[fl * 8 : fl * 8 + 8, 0:128]
            v = v + jnp.where(row == 0, r_next[fl : fl + 1], 0.0) + jnp.where(row == 7, r_prev[fl : fl + 1], 0.0)
            m.append(v + jnp.where(keep, pltpu.roll(side, 128 - fl, 1) if fl else side, 0.0))
        for k, (p, q) in enumerate(PAIRS):
            at = (k * LEV + lev) * 8
            s_ref[at : at + 8] = m[4 + k] - m[p] * m[q]
    half = iota((32, 128), 1) < 64
    tiles = []
    for tt in range(3):
        st = s_ref[tt * 128 : tt * 128 + 128].T
        rt = pltpu.roll(st, 64, 1)
        left = [st[i * 32 : i * 32 + 32] for i in range(4)]
        right = [rt[i * 32 : i * 32 + 32] for i in range(4)]
        tiles.append((jnp.where(half, left[0], right[1]), jnp.where(half, left[2], right[3])))
        tiles.append((jnp.where(half, right[0], left[1]), jnp.where(half, right[2], left[3])))
    tiles = tiles[:5]
    lhs = jnp.concatenate([jnp.concatenate([a, b], axis=1) for a, b in tiles], axis=0)
    lhs = jnp.concatenate(split3(lhs), axis=0)
    m_copy.wait()
    o = jnp.dot(lhs, m_ref[...], preferred_element_type=jnp.float32).astype(jnp.bfloat16)
    pay = []
    for part in range(3):
        for by in range(2):
            at = part * 160
            pay.append(jnp.concatenate(
                [o[at + gg * 32 : at + gg * 32 + 32, by * 128 : by * 128 + 128] for gg in range(5)], axis=1))
    pair = jnp.concatenate(pay[0:4], axis=0)
    one = jnp.concatenate(pay[4:6], axis=0)
    out = jnp.dot(sel, pair, preferred_element_type=jnp.float32)
    out = out + jnp.dot(sel[:, :64], one, preferred_element_type=jnp.float32)
    src[...] = out.reshape(n, 2, 640)

    own = pltpu.make_async_copy(src.at[me], dst.at[me], lsem)
    own.start()

    def send(k, carry):
        d = lax.rem(me + k, n)
        pltpu.make_async_remote_copy(
            src.at[d], dst.at[me], ssem, rsem, device_id=(d // n_gy, lax.rem(d, n_gy)), device_id_type=MESH
        ).start()
        return carry

    lax.fori_loop(1, n, send, 0)
    own.wait()
    rest = pl.ds(0, n - 1)
    pltpu.make_async_copy(src.at[rest], dst.at[rest], ssem).wait()
    pltpu.make_async_copy(src.at[rest], dst.at[rest], rsem).wait()


def per_device(fields, owner):
    n_gx, n_gy = lax.axis_size("gx"), lax.axis_size("gy")
    n = n_gx * n_gy
    taps = gauss_taps()
    g = [float(x) for x in taps]
    length = fields.shape[-1]
    weights = jnp.asarray(east_matrix(length, taps))
    blocks = jnp.asarray(block_matrix(), jnp.bfloat16)
    f32 = jnp.float32
    out = pl.pallas_call(
        functools.partial(kernel, n_gx, n_gy, g),
        out_shape=jax.ShapeDtypeStruct((n, 2, 640), f32),
        in_specs=[
            pl.BlockSpec(memory_space=pltpu.HBM),
            pl.BlockSpec(memory_space=pltpu.HBM),
            pl.BlockSpec(memory_space=pltpu.HBM),
            pl.BlockSpec(memory_space=pltpu.HBM),
        ],
        out_specs=pl.BlockSpec(memory_space=pltpu.VMEM),
        scratch_shapes=[
            pltpu.VMEM((length // 128, 4, LEV, 80, 128), f32),
            pltpu.VMEM((length // KC, KC, 256), f32),
            pltpu.VMEM((256, 256), jnp.bfloat16),
            pltpu.VMEM((1, 64), jnp.int32),
            pltpu.VMEM((ROWS, KC), f32),
            pltpu.VMEM((ROWS, 256), f32),
            pltpu.VMEM((384, 128), f32),
            pltpu.VMEM((n, 2, 640), f32),
            pltpu.VMEM((8, 128), f32),
            pltpu.VMEM((8, 128), f32),
            pltpu.VMEM((SIDE, 128), f32),
            pltpu.VMEM((SIDE, 128), f32),
            pltpu.VMEM((2, 8, 128), f32),
            pltpu.VMEM((4, 8, 128), f32),
            pltpu.SemaphoreType.DMA((length // 128,)),
            pltpu.SemaphoreType.DMA((length // KC,)),
            pltpu.SemaphoreType.DMA,
            pltpu.SemaphoreType.DMA,
            pltpu.SemaphoreType.DMA,
            pltpu.SemaphoreType.DMA,
            pltpu.SemaphoreType.DMA((8,)),
            pltpu.SemaphoreType.DMA((8,)),
            pltpu.SemaphoreType.DMA,
        ],
        compiler_params=pltpu.CompilerParams(
            collective_id=0, has_side_effects=True, vmem_limit_bytes=24 << 20
        ),
    )(*(pltpu.with_memory_space_constraint(x, pltpu.HBM) for x in (fields, weights, blocks, owner.reshape(1, 64))))
    return out.reshape(n * 2, 640)


def solution(mesh):
    placed = (P(None, None, "gy", "gx"), P(("gx", "gy"), None))
    return jax.shard_map(
        per_device, mesh=mesh, in_specs=placed, out_specs=P(("gx", "gy"), None), check_vma=False
    )
```

profile of v0, /device:TPU:25, one launch (start us, length us, event | category | flops | bytes accessed | tf_op | source)
XLA Modules:
  0.0 32.9 jit_solution(10534203465929621676)
XLA Ops:
  0.0 31.6 %shard_map.46 = f32[128,2,640]{2,1,0:T(2,128)S(1)} custom-call(f32[4,4,80,1280]{3,2,1,0:T(8,128)} %f_hbm.1, f32[1280,256]{1,0:T(8,128)} %constant.4.clone.w_hbm, bf16[256,256]{1,0:T(8,128)(2,1)} %constant.5.clone.m_hbm, s32[1,64]{1,0:T(1,128)} %bitcast.1), custom_call_target="tpu_custom_call" | custom-call | tf_op jit(solution)/shard_map/pallas_call | solution.py:260
  31.6 1.3 %reshape.7 = f32[256,640]{1,0:T(8,128)} reshape(f32[128,2,640]{2,1,0:T(2,128)S(1)} %shard_map.46) | data formatting | bytes 1310720 | tf_op jit(solution)/shard_map/reshape | solution.py:299
where the time goes:
time: 33 us; the launch traced here: 32.9 us
  Pallas kernels  31.6 us (96%)
  local copies, waits for them, and re-layouts  1.29 us (4%)
    pallas_call x1, Pallas kernels, per_device(): pl.pallas_call(functools.partial(kernel, n_gx, n_gy, g), out_shape=jax.Sh...  31.6 us
    reshape x1, local copies, waits for them, and re-layouts, per_device(): return out.reshape(n * 2, 640)  1.29 us

commit v1 on v0

v1 whole, which is shorter than its diff:
```python
import functools

import jax
import jax.numpy as jnp
import numpy as np
from jax import lax
from jax.experimental import pallas as pl
from jax.experimental.pallas import tpu as pltpu
from jax.sharding import PartitionSpec as P

MESH = pl.DeviceIdType.MESH
BLK = 4
LEV = 4
RATIO = 10
TAPS = 21
SIGMA_CELLS = 2.8867513
PAIRS = ((0, 0), (0, 1), (0, 2), (0, 3), (1, 1), (1, 2), (1, 3), (2, 2), (2, 3), (3, 3))
ROUND_A = tuple((a, None) for a in range(4)) + PAIRS[:4]
ROUND_B = PAIRS[4:]
SIDE = 32
KC = 256
ORDER = (0, 3, 1, 2)
LANE_LAST = 63


def gauss_taps():
    spread = np.arange(TAPS, dtype=np.float32) - np.float32(10.0)
    values = np.exp(-spread * spread / np.float32(2.0 * SIGMA_CELLS * SIGMA_CELLS)).astype(np.float32)
    return (values / values.sum(dtype=np.float32)).astype(np.float32)


def east_matrix(length, taps):
    coarse = length // RATIO
    w = np.zeros((length, 256), np.float32)
    cols = [(128, coarse), (128 + LANE_LAST, -1)]
    for lane in range(128):
        cols.append((lane, 4 * (lane % 32) + ORDER[lane // 32]))
    for lane, j in cols:
        for t in range(TAPS):
            x = RATIO * j - 5 + t
            if 0 <= x < length:
                w[x, lane] = taps[t]
    return w


def block_matrix():
    m = np.zeros((256, 256), np.float32)
    for grp in range(4):
        for kl in range(8):
            for i in range(8):
                by, r = divmod(i, 4)
                m[grp * 64 + kl * 8 + i, by * 128 + kl * 16 + r * 4 + ORDER[grp]] = 1.0
    return m


def split3(x):
    hi = x.astype(jnp.bfloat16)
    rest = x - hi.astype(jnp.float32)
    mid = rest.astype(jnp.bfloat16)
    lo = (rest - mid.astype(jnp.float32)).astype(jnp.bfloat16)
    return hi, mid, lo


def iota(shape, dim):
    return lax.broadcasted_iota(jnp.int32, shape, dim)


def north_parts(v, g):
    q5, q0 = g[5] * v[0], g[0] * v[5]
    a = q5 + g[10] * v[5] + g[9] * (v[4] + v[6]) + g[8] * (v[3] + v[7]) + g[7] * (v[2] + v[8]) + g[6] * (v[1] + v[9])
    b = q0 + g[1] * v[6] + g[2] * v[7] + g[3] * v[8] + g[4] * v[9]
    c = q5 + q0 + g[4] * v[1] + g[3] * v[2] + g[2] * v[3] + g[1] * v[4]
    return a, b, c


def north_chunk(fields, f_ref, kc, x_ref, g):
    row = iota((8, 128), 0)
    main = len(fields) * LEV * 8
    used = sorted({a for pair in fields for a in pair if a is not None})
    for lev in range(LEV):
        for lt in range(KC // 128):
            lanes = slice(lt * 128, lt * 128 + 128)
            x = {a: [f_ref[kc * (KC // 128) + lt, a, lev, pl.ds(o, 8, stride=RATIO), :] for o in range(RATIO)] for a in used}
            for f, (p, q) in enumerate(fields):
                v = x[p] if q is None else [x[p][o] * x[q][o] for o in range(RATIO)]
                a, b, c = north_parts(v, g)
                b = pltpu.roll(b, 1, 0)
                c = pltpu.roll(c, 7, 0)
                fl = f * LEV + lev
                x_ref[fl * 8 : fl * 8 + 8, lanes] = a + jnp.where(row == 0, 0.0, b) + jnp.where(row == 7, 0.0, c)
                x_ref[main + fl : main + fl + 1, lanes] = b[0:1]
                x_ref[main + SIDE + fl : main + SIDE + fl + 1, lanes] = c[7:8]


def selector(owner_ref):
    own = owner_ref[...].astype(jnp.float32)
    row = jnp.broadcast_to(jnp.concatenate([own, own], axis=1), (128, 128))
    col = row.T[:64]
    before = (col == row[:64]) & (iota((64, 128), 0) < (iota((64, 128), 1) & 63))
    rank = jnp.sum(before.astype(jnp.float32), axis=0, keepdims=True)
    slot = row[0:1] * 2.0 + rank
    where = iota((256, 128), 0).astype(jnp.float32)
    return (where == slot).astype(jnp.bfloat16)


def pack_rim(count, t_ref, edge, corner):
    lane = iota((8, 128), 1)
    row = iota((8, 128), 0)
    keep = (lane == 0) | (lane == LANE_LAST)
    packed = jnp.zeros((8, 128), jnp.float32)
    for fl in range(count):
        v = jnp.where(keep, t_ref[fl * 8 : fl * 8 + 8, 128:256], 0.0)
        packed = packed + (pltpu.roll(v, fl, 1) if fl else v)
    edge[...] = packed
    rows = count * 8 + 2 * SIDE
    turned = t_ref[rows - 128 : rows, 128:256].T
    corner[...] = jnp.where(row == 0, turned[0:1], turned[LANE_LAST : LANE_LAST + 1])


def rim_copies(n_gx, n_gy, gx, gy, count, t_ref, edge, corner, r_next, r_prev, r_side, r_corner, hsend, hrecv):
    east, west = lax.rem(gx + 1, n_gx), lax.rem(gx + n_gx - 1, n_gx)
    up, down = lax.rem(gy + 1, n_gy), lax.rem(gy + n_gy - 1, n_gy)
    main = count * 8
    moves = (
        (t_ref.at[main : main + SIDE, 0:128], r_next, (gx, up)),
        (t_ref.at[main + SIDE : main + 2 * SIDE, 0:128], r_prev, (gx, down)),
        (edge, r_side.at[0], (east, gy)),
        (edge, r_side.at[1], (west, gy)),
        (corner, r_corner.at[0], (east, up)),
        (corner, r_corner.at[1], (east, down)),
        (corner, r_corner.at[2], (west, up)),
        (corner, r_corner.at[3], (west, down)),
    )
    return [
        pltpu.make_async_remote_copy(s, d, hsend.at[i], hrecv.at[i], device_id=to, device_id_type=MESH)
        for i, (s, d, to) in enumerate(moves)
    ]


def rim_added(count, t_ref, r_next, r_prev, r_side, r_corner):
    lane = iota((8, 128), 1)
    row = iota((8, 128), 0)
    keep = (lane == 0) | (lane == LANE_LAST)
    side = jnp.where(lane < 60, r_side[0], r_side[1])
    first = lane < count
    secnd = (lane >= LANE_LAST) & (lane < LANE_LAST + count)
    corners = ((first, 0, 0, 64), (first, 7, 0, 32), (secnd, 0, 1, 127), (secnd, 7, 1, 95))
    for i, (lanes, at, got, turn) in enumerate(corners):
        v = jnp.broadcast_to(r_corner[i, got : got + 1], (8, 128))
        side = side + jnp.where(lanes & (row == at), pltpu.roll(v, turn, 1), 0.0)
    out = []
    for fl in range(count):
        v = t_ref[fl * 8 : fl * 8 + 8, 0:128]
        v = v + jnp.where(row == 0, r_next[fl : fl + 1], 0.0) + jnp.where(row == 7, r_prev[fl : fl + 1], 0.0)
        out.append(v + jnp.where(keep, pltpu.roll(side, 128 - fl, 1) if fl else side, 0.0))
    return out


def slots(groups, sel, s_ref, m_ref):
    half = iota((32, 128), 1) < 64
    tiles = []
    for tt in range((groups + 1) // 2):
        st = s_ref[tt * 128 : tt * 128 + 128].T
        rt = pltpu.roll(st, 64, 1)
        left = [st[i * 32 : i * 32 + 32] for i in range(4)]
        right = [rt[i * 32 : i * 32 + 32] for i in range(4)]
        tiles.append((jnp.where(half, left[0], right[1]), jnp.where(half, left[2], right[3])))
        tiles.append((jnp.where(half, right[0], left[1]), jnp.where(half, right[2], left[3])))
    tiles = tiles[:groups]
    lhs = jnp.concatenate([jnp.concatenate([a, b], axis=1) for a, b in tiles], axis=0)
    lhs = jnp.concatenate(split3(lhs), axis=0)
    o = jnp.dot(lhs, m_ref[...], preferred_element_type=jnp.float32).astype(jnp.bfloat16)
    pay = []
    for part in range(3):
        for by in range(2):
            at = part * groups * 32
            pay.append(jnp.concatenate(
                [o[at + gg * 32 : at + gg * 32 + 32, by * 128 : by * 128 + 128] for gg in range(groups)], axis=1))
    out = jnp.dot(sel, jnp.concatenate(pay[0:4], axis=0), preferred_element_type=jnp.float32)
    return out + jnp.dot(sel[:, :64], jnp.concatenate(pay[4:6], axis=0), preferred_element_type=jnp.float32)


def kernel(n_gx, n_gy, g, f_hbm, w_hbm, m_hbm, o_hbm, out_ref, f_ref, w_ref, m_ref, owner_ref, x_a, x_b, t_a, t_b,
           mean_ref, s_a, s_b, src_a, src_b, dst_a, dst_b, edge, corner, r_next, r_prev, r_side, r_corner,
           fsem, wsem, msem, osem, ssem, rsem, hsend, hrecv, lsem):
    n = n_gx * n_gy
    gx, gy = lax.axis_index("gx"), lax.axis_index("gy")
    me = gx * n_gy + gy
    steps = w_ref.shape[0]
    per = KC // 128
    count_a, count_b = len(ROUND_A) * LEV, len(ROUND_B) * LEV

    def f_copy(lt):
        return pltpu.make_async_copy(f_hbm.at[:, :, :, pl.ds(pl.multiple_of(lt * 128, 128), 128)], f_ref.at[lt], fsem.at[lt])

    def w_copy(kc):
        return pltpu.make_async_copy(w_hbm.at[pl.ds(pl.multiple_of(kc * KC, KC), KC)], w_ref.at[kc], wsem.at[kc])

    for kc in range(steps):
        for lt in range(per):
            f_copy(kc * per + lt).start()
        w_copy(kc).start()
    m_copy = pltpu.make_async_copy(m_hbm, m_ref, msem)
    m_copy.start()
    o_copy = pltpu.make_async_copy(o_hbm, owner_ref, osem)
    o_copy.start()

    barrier = pltpu.get_barrier_semaphore()

    def greet(k, carry):
        d = lax.rem(me + k, n)
        pl.semaphore_signal(barrier, inc=1, device_id=(d // n_gy, lax.rem(d, n_gy)), device_id_type=MESH)
        return carry

    lax.fori_loop(1, n, greet, 0)

    def local(fields, x_ref, t_ref, fresh):
        main = len(fields) * LEV * 8
        x_ref[main : main + 2 * SIDE] = jnp.zeros((2 * SIDE, KC), jnp.float32)
        t_ref[...] = jnp.zeros_like(t_ref)

        def chunk(kc, carry):
            if fresh:
                for lt in range(per):
                    f_copy(kc * per + lt).wait()
            north_chunk(fields, f_ref, kc, x_ref, g)
            if fresh:
                w_copy(kc).wait()
            t_ref[...] += jnp.dot(
                x_ref[...], w_ref[kc], precision=lax.Precision.HIGHEST, preferred_element_type=jnp.float32)
            return carry

        lax.fori_loop(0, steps, chunk, 0)

    def rims(i, count, t_ref):
        bufs = (edge, corner, r_next, r_prev, r_side, r_corner, hsend, hrecv)
        return rim_copies(n_gx, n_gy, gx, gy, count, t_ref, *(b.at[i] for b in bufs))

    def hand_over(i, src, dst):
        own = pltpu.make_async_copy(src.at[me], dst.at[me], lsem.at[i])
        own.start()

        def send(k, carry):
            d = lax.rem(me + k, n)
            pltpu.make_async_remote_copy(
                src.at[d], dst.at[me], ssem.at[i], rsem.at[i],
                device_id=(d // n_gy, lax.rem(d, n_gy)), device_id_type=MESH,
            ).start()
            return carry

        lax.fori_loop(1, n, send, 0)
        return own

    local(ROUND_A, x_a, t_a, True)
    pack_rim(count_a, t_a, edge.at[0], corner.at[0])
    pl.semaphore_wait(barrier, n - 1)
    copies_a = rims(0, count_a, t_a)
    for copy in copies_a:
        copy.start()
    local(ROUND_B, x_b, t_b, False)
    pack_rim(count_b, t_b, edge.at[1], corner.at[1])
    copies_b = rims(1, count_b, t_b)
    for copy in copies_b:
        copy.start()
    o_copy.wait()
    m_copy.wait()
    sel = selector(owner_ref)

    for copy in copies_a:
        copy.wait()
    got = rim_added(count_a, t_a, r_next.at[0], r_prev.at[0], r_side.at[0], r_corner.at[0])
    for fl in range(4 * LEV):
        mean_ref[fl] = got[fl]
    for k in range(4):
        for lev in range(LEV):
            p, q = PAIRS[k]
            s_a[(k * LEV + lev) * 8 : (k * LEV + lev) * 8 + 8] = (
                got[(4 + k) * LEV + lev] - got[p * LEV + lev] * got[q * LEV + lev])
    src_a[...] = slots(2, sel, s_a, m_ref).reshape(n, 2, 256)
    own_a = hand_over(0, src_a, dst_a)

    for copy in copies_b:
        copy.wait()
    got = rim_added(count_b, t_b, r_next.at[1], r_prev.at[1], r_side.at[1], r_corner.at[1])
    for k in range(len(ROUND_B)):
        for lev in range(LEV):
            p, q = ROUND_B[k]
            s_b[(k * LEV + lev) * 8 : (k * LEV + lev) * 8 + 8] = (
                got[k * LEV + lev] - mean_ref[p * LEV + lev] * mean_ref[q * LEV + lev])
    src_b[...] = slots(3, sel, s_b, m_ref).reshape(n, 2, 384)
    own_b = hand_over(1, src_b, dst_b)

    rest = pl.ds(0, n - 1)
    own_a.wait()
    pltpu.make_async_copy(dst_a.at[rest], dst_a.at[rest], rsem.at[0]).wait()
    out_ref[:, 0:256] = dst_a[...].reshape(2 * n, 256)
    own_b.wait()
    pltpu.make_async_copy(dst_b.at[rest], dst_b.at[rest], rsem.at[1]).wait()
    out_ref[:, 256:640] = dst_b[...].reshape(2 * n, 384)
    pltpu.make_async_copy(src_a.at[rest], src_a.at[rest], ssem.at[0]).wait()
    pltpu.make_async_copy(src_b.at[rest], src_b.at[rest], ssem.at[1]).wait()


def per_device(fields, owner):
    n_gx, n_gy = lax.axis_size("gx"), lax.axis_size("gy")
    n = n_gx * n_gy
    taps = gauss_taps()
    g = [float(x) for x in taps]
    length = fields.shape[-1]
    weights = jnp.asarray(east_matrix(length, taps))
    blocks = jnp.asarray(block_matrix(), jnp.bfloat16)
    f32 = jnp.float32
    rows_a, rows_b = (len(r) * LEV * 8 + 2 * SIDE for r in (ROUND_A, ROUND_B))
    return pl.pallas_call(
        functools.partial(kernel, n_gx, n_gy, g),
        out_shape=jax.ShapeDtypeStruct((2 * n, 640), f32),
        in_specs=[pl.BlockSpec(memory_space=pltpu.HBM)] * 4,
        out_specs=pl.BlockSpec(memory_space=pltpu.VMEM),
        scratch_shapes=[
            pltpu.VMEM((length // 128, 4, LEV, 80, 128), f32),
            pltpu.VMEM((length // KC, KC, 256), f32),
            pltpu.VMEM((256, 256), jnp.bfloat16),
            pltpu.VMEM((1, 64), jnp.int32),
            pltpu.VMEM((rows_a, KC), f32),
            pltpu.VMEM((rows_b, KC), f32),
            pltpu.VMEM((rows_a, 256), f32),
            pltpu.VMEM((rows_b, 256), f32),
            pltpu.VMEM((4 * LEV, 8, 128), f32),
            pltpu.VMEM((128, 128), f32),
            pltpu.VMEM((256, 128), f32),
            pltpu.VMEM((n, 2, 256), f32),
            pltpu.VMEM((n, 2, 384), f32),
            pltpu.VMEM((n, 2, 256), f32),
            pltpu.VMEM((n, 2, 384), f32),
            pltpu.VMEM((2, 8, 128), f32),
            pltpu.VMEM((2, 8, 128), f32),
            pltpu.VMEM((2, SIDE, 128), f32),
            pltpu.VMEM((2, SIDE, 128), f32),
            pltpu.VMEM((2, 2, 8, 128), f32),
            pltpu.VMEM((2, 4, 8, 128), f32),
            pltpu.SemaphoreType.DMA((length // 128,)),
            pltpu.SemaphoreType.DMA((length // KC,)),
            pltpu.SemaphoreType.DMA,
            pltpu.SemaphoreType.DMA,
            pltpu.SemaphoreType.DMA((2,)),
            pltpu.SemaphoreType.DMA((2,)),
            pltpu.SemaphoreType.DMA((2, 8)),
            pltpu.SemaphoreType.DMA((2, 8)),
            pltpu.SemaphoreType.DMA((2,)),
        ],
        compiler_params=pltpu.CompilerParams(
            collective_id=0, has_side_effects=True, vmem_limit_bytes=24 << 20
        ),
    )(*(pltpu.with_memory_space_constraint(x, pltpu.HBM) for x in (fields, weights, blocks, owner.reshape(1, 64))))


def solution(mesh):
    placed = (P(None, None, "gy", "gx"), P(("gx", "gy"), None))
    return jax.shard_map(
        per_device, mesh=mesh, in_specs=placed, out_specs=P(("gx", "gy"), None), check_vma=False
    )
```

time: 33 us -> 30.7 us (0.930)
  the two profiles are of different devices: /device:TPU:25 before, /device:TPU:1 now
where the time goes in v1:
time: 30.7 us; the launch traced here: 30.6 us
  Pallas kernels  29.8 us (97%)
  local copies, waits for them, and re-layouts  0.84 us (3%)
    pallas_call x1, Pallas kernels, per_device(): pl.pallas_call(functools.partial(kernel, n_gx, n_gy, g), out_shape=jax.Sh...  29.8 us
    unnamed x1, local copies, waits for them, and re-layouts  0.84 us

profile of v1, /device:TPU:1, one launch (start us, length us, event | category | flops | bytes accessed | tf_op | source)
XLA Modules:
  0.0 30.6 jit_solution(7128260046851894030)
XLA Ops:
  0.0 29.8 %shard_map.46 = f32[256,640]{1,0:T(8,128)S(1)} custom-call(f32[4,4,80,1280]{3,2,1,0:T(8,128)} %f_hbm.1, f32[1280,256]{1,0:T(8,128)} %constant.4.clone.w_hbm, bf16[256,256]{1,0:T(8,128)(2,1)} %constant.5.clone.m_hbm, s32[1,64]{1,0:T(1,128)} %bitcast.1), custom_call_target="tpu_custom_call" | custom-call | tf_op jit(solution)/shard_map/pallas_call | solution.py:314
  29.8 0.8 %copy.6 = f32[256,640]{1,0:T(8,128)} copy(f32[256,640]{1,0:T(8,128)S(1)} %shard_map.46) | data formatting | bytes 1310720

commit v2 on v1

--- a/solution.py
+++ b/solution.py
@@ -9,16 +9,18 @@
 from jax.sharding import PartitionSpec as P
 
 MESH = pl.DeviceIdType.MESH
+LOGICAL = pl.DeviceIdType.LOGICAL
 BLK = 4
+FIRST = 4
 LEV = 4
 RATIO = 10
 TAPS = 21
 SIGMA_CELLS = 2.8867513
 PAIRS = ((0, 0), (0, 1), (0, 2), (0, 3), (1, 1), (1, 2), (1, 3), (2, 2), (2, 3), (3, 3))
-ROUND_A = tuple((a, None) for a in range(4)) + PAIRS[:4]
-ROUND_B = PAIRS[4:]
-SIDE = 32
+ROUND_A = tuple((a, None) for a in range(4)) + PAIRS[:FIRST]
+ROUND_B = PAIRS[FIRST:]
 KC = 256
+AHEAD = 2
 ORDER = (0, 3, 1, 2)
 LANE_LAST = 63
 
@@ -43,6 +45,15 @@
     return w
 
 
+def east_parts(w):
+    parts = []
+    for _ in range(3):
+        parts.append(w.astype(jnp.bfloat16))
+        w = w - parts[-1].astype(np.float32)
+    hi, mid, lo = (p.reshape(-1, 1, KC, 256) for p in parts)
+    return np.concatenate([hi, mid, lo], axis=1)
+
+
 def block_matrix():
     m = np.zeros((256, 256), np.float32)
     for grp in range(4):
@@ -61,6 +72,26 @@
     return hi, mid, lo
 
 
+def east(x, w_ref):
+    rows = x.shape[0]
+    parts = jnp.concatenate(split3(x), axis=0)
+    out = None
+    for i in range(3):
+        p = jnp.dot(parts[: (3 - i) * rows], w_ref[i], preferred_element_type=jnp.float32)
+        for j in range(3 - i):
+            v = p[j * rows : j * rows + rows]
+            out = v if out is None else out + v
+    return out
+
+
+def side_rows(fields):
+    return -(-len(fields) * LEV // 8) * 8
+
+
+def places(fields):
+    return [(lev * len(fields) + f,) * 2 for lev in range(LEV) for f in range(len(fields))]
+
+
 def iota(shape, dim):
     return lax.broadcasted_iota(jnp.int32, shape, dim)
 
@@ -75,21 +106,25 @@
 
 def north_chunk(fields, f_ref, kc, x_ref, g):
     row = iota((8, 128), 0)
-    main = len(fields) * LEV * 8
+    main, side = len(fields) * LEV * 8, side_rows(fields)
     used = sorted({a for pair in fields for a in pair if a is not None})
+
+    def piece(lev, lt, lanes):
+        x = {a: [f_ref[kc * (KC // 128) + lt, a, lev, pl.ds(o, 8, stride=RATIO), :] for o in range(RATIO)] for a in used}
+        for f, (p, q) in enumerate(fields):
+            v = x[p] if q is None else [x[p][o] * x[q][o] for o in range(RATIO)]
+            a, b, c = north_parts(v, g)
+            b = pltpu.roll(b, 1, 0)
+            c = pltpu.roll(c, 7, 0)
+            at = (lev * len(fields) + f) * 8
+            x_ref[pl.ds(at, 8), lanes] = a + jnp.where(row == 0, 0.0, b) + jnp.where(row == 7, 0.0, c)
+            up = main + lev * len(fields) + f
+            x_ref[up : up + 1, lanes] = b[0:1]
+            x_ref[up + side : up + side + 1, lanes] = c[7:8]
+
     for lev in range(LEV):
         for lt in range(KC // 128):
-            lanes = slice(lt * 128, lt * 128 + 128)
-            x = {a: [f_ref[kc * (KC // 128) + lt, a, lev, pl.ds(o, 8, stride=RATIO), :] for o in range(RATIO)] for a in used}
-            for f, (p, q) in enumerate(fields):
-                v = x[p] if q is None else [x[p][o] * x[q][o] for o in range(RATIO)]
-                a, b, c = north_parts(v, g)
-                b = pltpu.roll(b, 1, 0)
-                c = pltpu.roll(c, 7, 0)
-                fl = f * LEV + lev
-                x_ref[fl * 8 : fl * 8 + 8, lanes] = a + jnp.where(row == 0, 0.0, b) + jnp.where(row == 7, 0.0, c)
-                x_ref[main + fl : main + fl + 1, lanes] = b[0:1]
-                x_ref[main + SIDE + fl : main + SIDE + fl + 1, lanes] = c[7:8]
+            piece(lev, lt, slice(lt * 128, lt * 128 + 128))
 
 
 def selector(owner_ref):
@@ -103,27 +138,27 @@
     return (where == slot).astype(jnp.bfloat16)
 
 
-def pack_rim(count, t_ref, edge, corner):
+def pack_rim(fields, t_ref, edge, corner):
     lane = iota((8, 128), 1)
     row = iota((8, 128), 0)
     keep = (lane == 0) | (lane == LANE_LAST)
     packed = jnp.zeros((8, 128), jnp.float32)
-    for fl in range(count):
-        v = jnp.where(keep, t_ref[fl * 8 : fl * 8 + 8, 128:256], 0.0)
-        packed = packed + (pltpu.roll(v, fl, 1) if fl else v)
+    for at, sl in places(fields):
+        v = jnp.where(keep, t_ref[at * 8 : at * 8 + 8, 128:256], 0.0)
+        packed = packed + (pltpu.roll(v, sl, 1) if sl else v)
     edge[...] = packed
-    rows = count * 8 + 2 * SIDE
+    rows = len(fields) * LEV * 8 + 2 * side_rows(fields)
     turned = t_ref[rows - 128 : rows, 128:256].T
     corner[...] = jnp.where(row == 0, turned[0:1], turned[LANE_LAST : LANE_LAST + 1])
 
 
-def rim_copies(n_gx, n_gy, gx, gy, count, t_ref, edge, corner, r_next, r_prev, r_side, r_corner, hsend, hrecv):
+def rim_copies(n_gx, n_gy, gx, gy, fields, t_ref, edge, corner, r_next, r_prev, r_side, r_corner, hsend, hrecv):
     east, west = lax.rem(gx + 1, n_gx), lax.rem(gx + n_gx - 1, n_gx)
     up, down = lax.rem(gy + 1, n_gy), lax.rem(gy + n_gy - 1, n_gy)
-    main = count * 8
+    main, n_side = len(fields) * LEV * 8, side_rows(fields)
     moves = (
-        (t_ref.at[main : main + SIDE, 0:128], r_next, (gx, up)),
-        (t_ref.at[main + SIDE : main + 2 * SIDE, 0:128], r_prev, (gx, down)),
+        (t_ref.at[main : main + n_side, 0:128], r_next.at[:n_side], (gx, up)),
+        (t_ref.at[main + n_side : main + 2 * n_side, 0:128], r_prev.at[:n_side], (gx, down)),
         (edge, r_side.at[0], (east, gy)),
         (edge, r_side.at[1], (west, gy)),
         (corner, r_corner.at[0], (east, up)),
@@ -137,22 +172,28 @@
     ]
 
 
-def rim_added(count, t_ref, r_next, r_prev, r_side, r_corner):
+def rim_added(fields, t_ref, r_next, r_prev, r_side, r_corner):
     lane = iota((8, 128), 1)
     row = iota((8, 128), 0)
     keep = (lane == 0) | (lane == LANE_LAST)
-    side = jnp.where(lane < 60, r_side[0], r_side[1])
-    first = lane < count
-    secnd = (lane >= LANE_LAST) & (lane < LANE_LAST + count)
-    corners = ((first, 0, 0, 64), (first, 7, 0, 32), (secnd, 0, 1, 127), (secnd, 7, 1, 95))
+    side = jnp.where(lane < LANE_LAST, r_side[0], r_side[1])
+    n_side = side_rows(fields)
+    first = lane < n_side
+    secnd = (lane >= LANE_LAST) & (lane < LANE_LAST + n_side)
+    corners = (
+        (first, 0, 0, 2 * n_side % 128),
+        (first, 7, 0, n_side),
+        (secnd, 0, 1, (LANE_LAST + 2 * n_side) % 128),
+        (secnd, 7, 1, (LANE_LAST + n_side) % 128),
+    )
     for i, (lanes, at, got, turn) in enumerate(corners):
         v = jnp.broadcast_to(r_corner[i, got : got + 1], (8, 128))
         side = side + jnp.where(lanes & (row == at), pltpu.roll(v, turn, 1), 0.0)
     out = []
-    for fl in range(count):
-        v = t_ref[fl * 8 : fl * 8 + 8, 0:128]
-        v = v + jnp.where(row == 0, r_next[fl : fl + 1], 0.0) + jnp.where(row == 7, r_prev[fl : fl + 1], 0.0)
-        out.append(v + jnp.where(keep, pltpu.roll(side, 128 - fl, 1) if fl else side, 0.0))
+    for at, sl in places(fields):
+        v = t_ref[at * 8 : at * 8 + 8, 0:128]
+        v = v + jnp.where(row == 0, r_next[sl : sl + 1], 0.0) + jnp.where(row == 7, r_prev[sl : sl + 1], 0.0)
+        out.append(v + jnp.where(keep, pltpu.roll(side, 128 - sl, 1) if sl else side, 0.0))
     return out
 
 
@@ -188,18 +229,21 @@
     me = gx * n_gy + gy
     steps = w_ref.shape[0]
     per = KC // 128
-    count_a, count_b = len(ROUND_A) * LEV, len(ROUND_B) * LEV
+    wide = FIRST * 64
 
     def f_copy(lt):
         return pltpu.make_async_copy(f_hbm.at[:, :, :, pl.ds(pl.multiple_of(lt * 128, 128), 128)], f_ref.at[lt], fsem.at[lt])
 
     def w_copy(kc):
-        return pltpu.make_async_copy(w_hbm.at[pl.ds(pl.multiple_of(kc * KC, KC), KC)], w_ref.at[kc], wsem.at[kc])
-
-    for kc in range(steps):
+        return pltpu.make_async_copy(w_hbm.at[kc], w_ref.at[kc], wsem.at[kc])
+
+    def fetch(kc):
         for lt in range(per):
             f_copy(kc * per + lt).start()
         w_copy(kc).start()
+
+    for kc in range(AHEAD):
+        fetch(kc)
     m_copy = pltpu.make_async_copy(m_hbm, m_ref, msem)
     m_copy.start()
     o_copy = pltpu.make_async_copy(o_hbm, owner_ref, osem)
@@ -209,32 +253,33 @@
 
     def greet(k, carry):
         d = lax.rem(me + k, n)
-        pl.semaphore_signal(barrier, inc=1, device_id=(d // n_gy, lax.rem(d, n_gy)), device_id_type=MESH)
+        pl.semaphore_signal(barrier, inc=1, device_id=d, device_id_type=LOGICAL)
         return carry
 
-    lax.fori_loop(1, n, greet, 0)
+    lax.fori_loop(1, n, greet, 0, unroll=8)
 
     def local(fields, x_ref, t_ref, fresh):
         main = len(fields) * LEV * 8
-        x_ref[main : main + 2 * SIDE] = jnp.zeros((2 * SIDE, KC), jnp.float32)
+        n_side = side_rows(fields)
+        x_ref[main : main + 2 * n_side] = jnp.zeros((2 * n_side, KC), jnp.float32)
         t_ref[...] = jnp.zeros_like(t_ref)
 
         def chunk(kc, carry):
             if fresh:
                 for lt in range(per):
                     f_copy(kc * per + lt).wait()
+                pl.when(kc + AHEAD < steps)(lambda: fetch(kc + AHEAD))
             north_chunk(fields, f_ref, kc, x_ref, g)
             if fresh:
                 w_copy(kc).wait()
-            t_ref[...] += jnp.dot(
-                x_ref[...], w_ref[kc], precision=lax.Precision.HIGHEST, preferred_element_type=jnp.float32)
+            t_ref[...] += east(x_ref[...], w_ref.at[kc])
             return carry
 
         lax.fori_loop(0, steps, chunk, 0)
 
-    def rims(i, count, t_ref):
+    def rims(i, fields, t_ref):
         bufs = (edge, corner, r_next, r_prev, r_side, r_corner, hsend, hrecv)
-        return rim_copies(n_gx, n_gy, gx, gy, count, t_ref, *(b.at[i] for b in bufs))
+        return rim_copies(n_gx, n_gy, gx, gy, fields, t_ref, *(b.at[i] for b in bufs))
 
     def hand_over(i, src, dst):
         own = pltpu.make_async_copy(src.at[me], dst.at[me], lsem.at[i])
@@ -244,22 +289,22 @@
             d = lax.rem(me + k, n)
             pltpu.make_async_remote_copy(
                 src.at[d], dst.at[me], ssem.at[i], rsem.at[i],
-                device_id=(d // n_gy, lax.rem(d, n_gy)), device_id_type=MESH,
+                device_id=d, device_id_type=LOGICAL,
             ).start()
             return carry
 
-        lax.fori_loop(1, n, send, 0)
+        lax.fori_loop(1, n, send, 0, unroll=8)
         return own
 
     local(ROUND_A, x_a, t_a, True)
-    pack_rim(count_a, t_a, edge.at[0], corner.at[0])
+    pack_rim(ROUND_A, t_a, edge.at[0], corner.at[0])
     pl.semaphore_wait(barrier, n - 1)
-    copies_a = rims(0, count_a, t_a)
+    copies_a = rims(0, ROUND_A, t_a)
     for copy in copies_a:
         copy.start()
     local(ROUND_B, x_b, t_b, False)
-    pack_rim(count_b, t_b, edge.at[1], corner.at[1])
-    copies_b = rims(1, count_b, t_b)
+    pack_rim(ROUND_B, t_b, edge.at[1], corner.at[1])
+    copies_b = rims(1, ROUND_B, t_b)
     for copy in copies_b:
         copy.start()
     o_copy.wait()
@@ -268,35 +313,36 @@
 
     for copy in copies_a:
         copy.wait()
-    got = rim_added(count_a, t_a, r_next.at[0], r_prev.at[0], r_side.at[0], r_corner.at[0])
-    for fl in range(4 * LEV):
-        mean_ref[fl] = got[fl]
-    for k in range(4):
+    got = rim_added(ROUND_A, t_a, r_next.at[0], r_prev.at[0], r_side.at[0], r_corner.at[0])
+    for lev in range(LEV):
+        for a in range(4):
+            mean_ref[lev * 4 + a] = got[lev * len(ROUND_A) + a]
+    for k in range(FIRST):
         for lev in range(LEV):
             p, q = PAIRS[k]
             s_a[(k * LEV + lev) * 8 : (k * LEV + lev) * 8 + 8] = (
-                got[(4 + k) * LEV + lev] - got[p * LEV + lev] * got[q * LEV + lev])
-    src_a[...] = slots(2, sel, s_a, m_ref).reshape(n, 2, 256)
+                got[lev * len(ROUND_A) + 4 + k] - got[lev * len(ROUND_A) + p] * got[lev * len(ROUND_A) + q])
+    src_a[...] = slots(FIRST // 2, sel, s_a, m_ref).reshape(n, 2, wide)
     own_a = hand_over(0, src_a, dst_a)
 
     for copy in copies_b:
         copy.wait()
-    got = rim_added(count_b, t_b, r_next.at[1], r_prev.at[1], r_side.at[1], r_corner.at[1])
+    got = rim_added(ROUND_B, t_b, r_next.at[1], r_prev.at[1], r_side.at[1], r_corner.at[1])
     for k in range(len(ROUND_B)):
         for lev in range(LEV):
             p, q = ROUND_B[k]
             s_b[(k * LEV + lev) * 8 : (k * LEV + lev) * 8 + 8] = (
-                got[k * LEV + lev] - mean_ref[p * LEV + lev] * mean_ref[q * LEV + lev])
-    src_b[...] = slots(3, sel, s_b, m_ref).reshape(n, 2, 384)
+                got[lev * len(ROUND_B) + k] - mean_ref[lev * 4 + p] * mean_ref[lev * 4 + q])
+    src_b[...] = slots(len(ROUND_B) // 2, sel, s_b, m_ref).reshape(n, 2, 640 - wide)
     own_b = hand_over(1, src_b, dst_b)
 
     rest = pl.ds(0, n - 1)
     own_a.wait()
     pltpu.make_async_copy(dst_a.at[rest], dst_a.at[rest], rsem.at[0]).wait()
-    out_ref[:, 0:256] = dst_a[...].reshape(2 * n, 256)
+    out_ref[:, :wide] = dst_a[...].reshape(2 * n, wide)
     own_b.wait()
     pltpu.make_async_copy(dst_b.at[rest], dst_b.at[rest], rsem.at[1]).wait()
-    out_ref[:, 256:640] = dst_b[...].reshape(2 * n, 384)
+    out_ref[:, wide:] = dst_b[...].reshape(2 * n, 640 - wide)
     pltpu.make_async_copy(src_a.at[rest], src_a.at[rest], ssem.at[0]).wait()
     pltpu.make_async_copy(src_b.at[rest], src_b.at[rest], ssem.at[1]).wait()
 
@@ -307,10 +353,12 @@
     taps = gauss_taps()
     g = [float(x) for x in taps]
     length = fields.shape[-1]
-    weights = jnp.asarray(east_matrix(length, taps))
+    weights = jnp.asarray(east_parts(east_matrix(length, taps)))
     blocks = jnp.asarray(block_matrix(), jnp.bfloat16)
     f32 = jnp.float32
-    rows_a, rows_b = (len(r) * LEV * 8 + 2 * SIDE for r in (ROUND_A, ROUND_B))
+    wide = FIRST * 64
+    side = side_rows(ROUND_A)
+    rows_a, rows_b = (len(r) * LEV * 8 + 2 * side_rows(r) for r in (ROUND_A, ROUND_B))
     return pl.pallas_call(
         functools.partial(kernel, n_gx, n_gy, g),
         out_shape=jax.ShapeDtypeStruct((2 * n, 640), f32),
@@ -318,7 +366,7 @@
         out_specs=pl.BlockSpec(memory_space=pltpu.VMEM),
         scratch_shapes=[
             pltpu.VMEM((length // 128, 4, LEV, 80, 128), f32),
-            pltpu.VMEM((length // KC, KC, 256), f32),
+            pltpu.VMEM((length // KC, 3, KC, 256), jnp.bfloat16),
             pltpu.VMEM((256, 256), jnp.bfloat16),
             pltpu.VMEM((1, 64), jnp.int32),
             pltpu.VMEM((rows_a, KC), f32),
@@ -326,16 +374,16 @@
             pltpu.VMEM((rows_a, 256), f32),
             pltpu.VMEM((rows_b, 256), f32),
             pltpu.VMEM((4 * LEV, 8, 128), f32),
-            pltpu.VMEM((128, 128), f32),
-            pltpu.VMEM((256, 128), f32),
-            pltpu.VMEM((n, 2, 256), f32),
-            pltpu.VMEM((n, 2, 384), f32),
-            pltpu.VMEM((n, 2, 256), f32),
-            pltpu.VMEM((n, 2, 384), f32),
+            pltpu.VMEM((-(-FIRST // 4) * 128, 128), f32),
+            pltpu.VMEM((-(-len(ROUND_B) // 4) * 128, 128), f32),
+            pltpu.VMEM((n, 2, wide), f32),
+            pltpu.VMEM((n, 2, 640 - wide), f32),
+            pltpu.VMEM((n, 2, wide), f32),
+            pltpu.VMEM((n, 2, 640 - wide), f32),
             pltpu.VMEM((2, 8, 128), f32),
             pltpu.VMEM((2, 8, 128), f32),
-            pltpu.VMEM((2, SIDE, 128), f32),
-            pltpu.VMEM((2, SIDE, 128), f32),
+            pltpu.VMEM((2, side, 128), f32),
+            pltpu.VMEM((2, side, 128), f32),
             pltpu.VMEM((2, 2, 8, 128), f32),
             pltpu.VMEM((2, 4, 8, 128), f32),
             pltpu.SemaphoreType.DMA((length // 128,)),

time: 30.7 us -> 28.5 us (0.928)
  Pallas kernels: 29.8 us -> 27.6 us
    pallas_call x1, Pallas kernels: 29.8 us -> 27.6 us  [per_device(): pl.pallas_call(functools.partial(kernel, n_gx, n_gy, g), out_shape=jax.Sh...]
where the time goes in v2:
time: 28.5 us; the launch traced here: 28.4 us
  Pallas kernels  27.6 us (97%)
  local copies, waits for them, and re-layouts  0.84 us (3%)
    pallas_call x1, Pallas kernels, per_device(): pl.pallas_call(functools.partial(kernel, n_gx, n_gy, g), out_shape=jax.Sh...  27.6 us
    unnamed x1, local copies, waits for them, and re-layouts  0.84 us

profile of v2, /device:TPU:1, one launch (start us, length us, event | category | flops | bytes accessed | tf_op | source)
XLA Modules:
  0.0 28.4 jit_solution(7353933749385570153)
XLA Ops:
  0.0 27.6 %shard_map.46 = f32[256,640]{1,0:T(8,128)S(1)} custom-call(f32[4,4,80,1280]{3,2,1,0:T(8,128)} %f_hbm.1, bf16[5,3,256,256]{3,2,1,0:T(8,128)(2,1)} %constant.4.clone.w_hbm, bf16[256,256]{1,0:T(8,128)(2,1)} %constant.5.clone.m_hbm, s32[1,64]{1,0:T(1,128)} %bitcast.1), custom_call_target="tpu_custom_call" | custom-call | tf_op jit(solution)/shard_map/pallas_call | solution.py:362
  27.6 0.8 %copy.6 = f32[256,640]{1,0:T(8,128)} copy(f32[256,640]{1,0:T(8,128)S(1)} %shard_map.46) | data formatting | bytes 1310720

commit v3 on v2

--- a/solution.py
+++ b/solution.py
@@ -20,7 +20,7 @@
 ROUND_A = tuple((a, None) for a in range(4)) + PAIRS[:FIRST]
 ROUND_B = PAIRS[FIRST:]
 KC = 256
-AHEAD = 2
+AHEAD = 3
 ORDER = (0, 3, 1, 2)
 LANE_LAST = 63
 
@@ -51,7 +51,9 @@
         parts.append(w.astype(jnp.bfloat16))
         w = w - parts[-1].astype(np.float32)
     hi, mid, lo = (p.reshape(-1, 1, KC, 256) for p in parts)
-    return np.concatenate([hi, mid, lo], axis=1)
+    rim = hi[..., 128:] + np.roll(mid[..., 128:], 1, -1) + np.roll(lo[..., 128:], 2, -1)
+    return np.concatenate(
+        [np.concatenate([hi[..., :128], mid[..., :128]], -1), np.concatenate([lo[..., :128], rim], -1)], axis=1)
 
 
 def block_matrix():
@@ -72,16 +74,17 @@
     return hi, mid, lo
 
 
-def east(x, w_ref):
+def east(x, w_ref, rim):
     rows = x.shape[0]
     parts = jnp.concatenate(split3(x), axis=0)
-    out = None
-    for i in range(3):
-        p = jnp.dot(parts[: (3 - i) * rows], w_ref[i], preferred_element_type=jnp.float32)
-        for j in range(3 - i):
-            v = p[j * rows : j * rows + rows]
-            out = v if out is None else out + v
-    return out
+    p = jnp.dot(parts, w_ref[0], preferred_element_type=jnp.float32)
+    q = jnp.dot(parts if rim else parts[:rows], w_ref[1], preferred_element_type=jnp.float32)
+    out = q[:rows, :128] + p[2 * rows :, :128] + p[rows : 2 * rows, 128:]
+    out = out + (p[rows : 2 * rows, :128] + p[:rows, 128:])
+    out = out + p[:rows, :128]
+    if not rim:
+        return out, None
+    return out, q[2 * rows :, 128:] + q[rows : 2 * rows, 128:] + q[:rows, 128:]
 
 
 def side_rows(fields):
@@ -135,7 +138,8 @@
     rank = jnp.sum(before.astype(jnp.float32), axis=0, keepdims=True)
     slot = row[0:1] * 2.0 + rank
     where = iota((256, 128), 0).astype(jnp.float32)
-    return (where == slot).astype(jnp.bfloat16)
+    sel = (where == slot).astype(jnp.bfloat16)
+    return jnp.concatenate([sel, sel[:, :64]], axis=1)
 
 
 def pack_rim(fields, t_ref, edge, corner):
@@ -217,11 +221,10 @@
             at = part * groups * 32
             pay.append(jnp.concatenate(
                 [o[at + gg * 32 : at + gg * 32 + 32, by * 128 : by * 128 + 128] for gg in range(groups)], axis=1))
-    out = jnp.dot(sel, jnp.concatenate(pay[0:4], axis=0), preferred_element_type=jnp.float32)
-    return out + jnp.dot(sel[:, :64], jnp.concatenate(pay[4:6], axis=0), preferred_element_type=jnp.float32)
-
-
-def kernel(n_gx, n_gy, g, f_hbm, w_hbm, m_hbm, o_hbm, out_ref, f_ref, w_ref, m_ref, owner_ref, x_a, x_b, t_a, t_b,
+    return jnp.dot(sel, jnp.concatenate(pay, axis=0), preferred_element_type=jnp.float32)
+
+
+def kernel(n_gx, n_gy, g, f_hbm, w_hbm, m_hbm, o_hbm, out_ref, f_ref, w_ref, m_ref, owner_ref, x_a, x_b, x_b1, t_a, t_b,
            mean_ref, s_a, s_b, src_a, src_b, dst_a, dst_b, edge, corner, r_next, r_prev, r_side, r_corner,
            fsem, wsem, msem, osem, ssem, rsem, hsend, hrecv, lsem):
     n = n_gx * n_gy
@@ -258,24 +261,42 @@
 
     lax.fori_loop(1, n, greet, 0, unroll=8)
 
-    def local(fields, x_ref, t_ref, fresh):
+    def local(fields, x_ref, t_ref, fresh, x_other=None):
         main = len(fields) * LEV * 8
         n_side = side_rows(fields)
-        x_ref[main : main + 2 * n_side] = jnp.zeros((2 * n_side, KC), jnp.float32)
+        for ref in (x_ref, x_other):
+            if ref is not None:
+                ref[main : main + 2 * n_side] = jnp.zeros((2 * n_side, KC), jnp.float32)
         t_ref[...] = jnp.zeros_like(t_ref)
 
+        def add(x, kc, rim):
+            part, side = east(x[...], w_ref.at[kc], rim)
+            t_ref[:, :128] += part
+            if rim:
+                t_ref[:, 128:] += side
+
         def chunk(kc, carry):
-            if fresh:
-                for lt in range(per):
-                    f_copy(kc * per + lt).wait()
-                pl.when(kc + AHEAD < steps)(lambda: fetch(kc + AHEAD))
+            for lt in range(per):
+                f_copy(kc * per + lt).wait()
+            pl.when(kc + AHEAD < steps)(lambda: fetch(kc + AHEAD))
             north_chunk(fields, f_ref, kc, x_ref, g)
-            if fresh:
-                w_copy(kc).wait()
-            t_ref[...] += east(x_ref[...], w_ref.at[kc])
+            w_copy(kc).wait()
+            rim = (kc == 0) | (kc == steps - 1)
+            pl.when(rim)(lambda: add(x_ref, kc, True))
+            pl.when(jnp.logical_not(rim))(lambda: add(x_ref, kc, False))
             return carry
 
-        lax.fori_loop(0, steps, chunk, 0)
+        if fresh:
+            lax.fori_loop(0, steps, chunk, 0)
+        else:
+            bufs = (x_ref, x_other)
+            for kc in range(steps):
+                north_chunk(fields, f_ref, kc, bufs[kc % 2], g)
+                if kc:
+                    add(bufs[(kc - 1) % 2], kc - 1, kc == 1)
+            add(bufs[(steps - 1) % 2], steps - 1, True)
+        side = t_ref[:, 128:]
+        t_ref[:, 128:] = side + pltpu.roll(side, 127, 1) + pltpu.roll(side, 126, 1)
 
     def rims(i, fields, t_ref):
         bufs = (edge, corner, r_next, r_prev, r_side, r_corner, hsend, hrecv)
@@ -286,7 +307,7 @@
         own.start()
 
         def send(k, carry):
-            d = lax.rem(me + k, n)
+            d = lax.rem(me + lax.rem(k, 4) * (n // 4) + lax.rem(k // 4, 4) * (n // 16) + k // 16, n)
             pltpu.make_async_remote_copy(
                 src.at[d], dst.at[me], ssem.at[i], rsem.at[i],
                 device_id=d, device_id_type=LOGICAL,
@@ -302,7 +323,7 @@
     copies_a = rims(0, ROUND_A, t_a)
     for copy in copies_a:
         copy.start()
-    local(ROUND_B, x_b, t_b, False)
+    local(ROUND_B, x_b, t_b, False, x_b1)
     pack_rim(ROUND_B, t_b, edge.at[1], corner.at[1])
     copies_b = rims(1, ROUND_B, t_b)
     for copy in copies_b:
@@ -366,10 +387,11 @@
         out_specs=pl.BlockSpec(memory_space=pltpu.VMEM),
         scratch_shapes=[
             pltpu.VMEM((length // 128, 4, LEV, 80, 128), f32),
-            pltpu.VMEM((length // KC, 3, KC, 256), jnp.bfloat16),
+            pltpu.VMEM((length // KC, 2, KC, 256), jnp.bfloat16),
             pltpu.VMEM((256, 256), jnp.bfloat16),
             pltpu.VMEM((1, 64), jnp.int32),
             pltpu.VMEM((rows_a, KC), f32),
+            pltpu.VMEM((rows_b, KC), f32),
             pltpu.VMEM((rows_b, KC), f32),
             pltpu.VMEM((rows_a, 256), f32),
             pltpu.VMEM((rows_b, 256), f32),

time: 28.5 us -> 28 us (0.982)
  Pallas kernels: 27.6 us -> 27.1 us
    pallas_call x1, Pallas kernels: 27.6 us -> 27.1 us  [per_device(): pl.pallas_call(functools.partial(kernel, n_gx, n_gy, g), out_shape=jax.Sh...]
where the time goes in v3:
time: 28 us; the launch traced here: 27.9 us
  Pallas kernels  27.1 us (97%)
  local copies, waits for them, and re-layouts  0.84 us (3%)
    pallas_call x1, Pallas kernels, per_device(): pl.pallas_call(functools.partial(kernel, n_gx, n_gy, g), out_shape=jax.Sh...  27.1 us
    unnamed x1, local copies, waits for them, and re-layouts  0.84 us

profile of v3, /device:TPU:1, one launch (start us, length us, event | category | flops | bytes accessed | tf_op | source)
XLA Modules:
  0.0 27.9 jit_solution(18187414170655331627)
XLA Ops:
  0.0 27.1 %shard_map.46 = f32[256,640]{1,0:T(8,128)S(1)} custom-call(f32[4,4,80,1280]{3,2,1,0:T(8,128)} %f_hbm.1, bf16[5,2,256,256]{3,2,1,0:T(8,128)(2,1)} %constant.4.clone.w_hbm, bf16[256,256]{1,0:T(8,128)(2,1)} %constant.5.clone.m_hbm, s32[1,64]{1,0:T(1,128)} %bitcast.1), custom_call_target="tpu_custom_call" | custom-call | tf_op jit(solution)/shard_map/pallas_call | solution.py:383
  27.1 0.8 %copy.6 = f32[256,640]{1,0:T(8,128)} copy(f32[256,640]{1,0:T(8,128)S(1)} %shard_map.46) | data formatting | bytes 1310720

commit v4 on v3

--- a/solution.py
+++ b/solution.py
@@ -259,7 +259,7 @@
         pl.semaphore_signal(barrier, inc=1, device_id=d, device_id_type=LOGICAL)
         return carry
 
-    lax.fori_loop(1, n, greet, 0, unroll=8)
+    lax.fori_loop(1, n, greet, 0, unroll=16)
 
     def local(fields, x_ref, t_ref, fresh, x_other=None):
         main = len(fields) * LEV * 8
@@ -323,15 +323,14 @@
     copies_a = rims(0, ROUND_A, t_a)
     for copy in copies_a:
         copy.start()
+    o_copy.wait()
+    m_copy.wait()
+    sel = selector(owner_ref)
     local(ROUND_B, x_b, t_b, False, x_b1)
     pack_rim(ROUND_B, t_b, edge.at[1], corner.at[1])
     copies_b = rims(1, ROUND_B, t_b)
     for copy in copies_b:
         copy.start()
-    o_copy.wait()
-    m_copy.wait()
-    sel = selector(owner_ref)
-
     for copy in copies_a:
         copy.wait()
     got = rim_added(ROUND_A, t_a, r_next.at[0], r_prev.at[0], r_side.at[0], r_corner.at[0])

time: 28 us -> 28 us (level)
  no operation moved by 1% of the time
where the time goes in v4:
time: 28 us; the launch traced here: 27.9 us
  Pallas kernels  27.1 us (97%)
  local copies, waits for them, and re-layouts  0.84 us (3%)
    pallas_call x1, Pallas kernels, per_device(): pl.pallas_call(functools.partial(kernel, n_gx, n_gy, g), out_shape=jax.Sh...  27.1 us
    unnamed x1, local copies, waits for them, and re-layouts  0.84 us

profile of v4, /device:TPU:1, one launch (start us, length us, event | category | flops | bytes accessed | tf_op | source)
XLA Modules:
  0.0 27.9 jit_solution(9336505430758976635)
XLA Ops:
  0.0 27.1 %shard_map.46 = f32[256,640]{1,0:T(8,128)S(1)} custom-call(f32[4,4,80,1280]{3,2,1,0:T(8,128)} %f_hbm.1, bf16[5,2,256,256]{3,2,1,0:T(8,128)(2,1)} %constant.4.clone.w_hbm, bf16[256,256]{1,0:T(8,128)(2,1)} %constant.5.clone.m_hbm, s32[1,64]{1,0:T(1,128)} %bitcast.1), custom_call_target="tpu_custom_call" | custom-call | tf_op jit(solution)/shard_map/pallas_call | solution.py:382
  27.1 0.8 %copy.6 = f32[256,640]{1,0:T(8,128)} copy(f32[256,640]{1,0:T(8,128)S(1)} %shard_map.46) | data formatting | bytes 1310720
